TPU v7x, 32 devices: a whole 2x2x4 slice. The times are simulated.
32 devices in a mesh: fsdp: 8 (over z, x), seq: 4 (over y, core).
Axes of the slice: x: 2, y: 2, z: 4, core: 2. Of those that a mesh axis runs over, the one named last changes fastest.
Arguments:
- tokens: bfloat16 [16384, 768], P(('fsdp', 'seq')), may hold values from -6 to 6
- read_memory: bfloat16 [8, 10, 768], P('fsdp'), may hold values from -6 to 6
- write_memory: bfloat16 [8, 10, 768], P('fsdp'), may hold values from -6 to 6
- lengths: int32 [8], P('fsdp'), may hold values from 1024 to 2048, as said below
- qkv_weight: bfloat16 [768, 2304], P('fsdp'), may hold values from -0.21875 to 0.21875
- qv_bias: bfloat16 [1536], P('fsdp'), may hold values from -1.5 to 1.5
- out_weight: bfloat16 [768, 768], P('fsdp'), may hold values from -6 to 6
- out_bias: bfloat16 [768], P('fsdp'), may hold values from -1.5 to 1.5
- norm1_gain: bfloat16 [768], P('fsdp'), may hold values from 0.5 to 1.5
- norm1_bias: bfloat16 [768], P('fsdp'), may hold values from -1.5 to 1.5
- up_weight: bfloat16 [768, 3072], P('fsdp'), may hold values from -0.21875 to 0.21875
- up_bias: bfloat16 [3072], P('fsdp'), may hold values from -1.5 to 1.5
- down_weight: bfloat16 [3072, 768], P('fsdp'), may hold values from -0.109375 to 0.109375
- down_bias: bfloat16 [768], P('fsdp'), may hold values from -1.5 to 1.5
- norm2_gain: bfloat16 [768], P('fsdp'), may hold values from 0.5 to 1.5
- norm2_bias: bfloat16 [768], P('fsdp'), may hold values from -1.5 to 1.5
- cotangent: bfloat16 [16384, 768], P(('fsdp', 'seq')), may hold values from -6 to 6
Outputs:
- output: bfloat16 [16384, 768], P(('fsdp', 'seq'))
- input_grad: float32 [16384, 768], P(('fsdp', 'seq'))
- read_grad: float32 [8, 10, 768], P('fsdp')
- write_grad: float32 [8, 10, 768], P('fsdp')
- qkv_weight_grad: float32 [768, 2304], P('fsdp')
- qv_bias_grad: float32 [1536], P('fsdp')
- out_weight_grad: float32 [768, 768], P('fsdp')
- out_bias_grad: float32 [768], P('fsdp')
- norm1_gain_grad: float32 [768], P('fsdp')
- norm1_bias_grad: float32 [768], P('fsdp')
- up_weight_grad: float32 [768, 3072], P('fsdp')
- up_bias_grad: float32 [3072], P('fsdp')
- down_weight_grad: float32 [3072, 768], P('fsdp')
- down_bias_grad: float32 [768], P('fsdp')
- norm2_gain_grad: float32 [768], P('fsdp')
- norm2_bias_grad: float32 [768], P('fsdp')
Inputs may be any that keep to these rules, and one draw needn't show every extreme that they name: `lengths`: valid length of each slot in positions, counting its 10 read and 10 write memory tokens; in every draw some slot has length 2048 and some slot 1024.
All inputs are finite; a program needn't handle non-finite values.
Results may differ from a plain program's by a relative error of at most 0.017.
Values may be sent and summed in bfloat16 or wider, within the bound.
A program may use at most 128 MiB of HBM per device.

v0:
```python
from functools import partial
import jax
import jax.numpy as jnp
from jax import lax
from jax.sharding import PartitionSpec as P

HEAD = 64
MEM = 10
norm_epsilon = 1e-06
masked_score = -1e30


def normalize(values, gain_vec, shift_vec):
    centre = values - jnp.mean(values, axis=-1, keepdims=True)
    factor = lax.rsqrt(jnp.mean(centre * centre, axis=-1, keepdims=True) + norm_epsilon)
    return centre * factor * gain_vec + shift_vec


def over_rows(left, right):
    return lax.dot_general(
        left, right, (((0,), (0,)), ((), ())), preferred_element_type=jnp.float32
    )


def by_columns(left, right):
    return lax.dot_general(
        left, right, (((1,), (1,)), ((), ())), preferred_element_type=jnp.float32
    )


def column_sums(values):
    return jnp.sum(values, axis=0, dtype=jnp.float32)


def per_device(
    tokens,
    read_memory,
    write_memory,
    lengths,
    qkv_weight,
    qv_bias,
    out_weight,
    out_bias,
    norm1_gain,
    norm1_bias,
    up_weight,
    up_bias,
    down_weight,
    down_bias,
    norm2_gain,
    norm2_bias,
    cotangent,
):
    seq_count = lax.axis_size("seq")
    local_rows = tokens.shape[0]
    model_width = tokens.shape[1]
    slot_rows = local_rows * seq_count
    head_cols = model_width // seq_count
    head_count = head_cols // HEAD
    block_rows = min(512, slot_rows)
    block_count = slot_rows // block_rows
    factor = HEAD ** (-0.5)
    length = lengths[0]
    places = lax.axis_index("seq") * local_rows + jnp.arange(local_rows, dtype=jnp.int32)
    in_slot = (places < length)[:, None]
    memory_slots = jnp.arange(MEM, dtype=jnp.int32)
    pick_read = places[:, None] == memory_slots[None, :]
    pick_write = places[:, None] == length - MEM + memory_slots[None, :]
    is_memory = jnp.any(pick_read | pick_write, axis=1)[:, None]
    read_float = pick_read.astype(jnp.float32)
    write_float = pick_write.astype(jnp.float32)
    memory_rows = jnp.dot(
        read_float.astype(jnp.bfloat16), read_memory[0], preferred_element_type=jnp.float32
    ) + jnp.dot(
        write_float.astype(jnp.bfloat16), write_memory[0], preferred_element_type=jnp.float32
    )
    layer_in = jnp.where(is_memory, memory_rows.astype(jnp.bfloat16), tokens)
    qkv_full, qv_full, out_full, out_bias_full, gain_one, shift_one = (
        lax.all_gather(qkv_weight, "fsdp", axis=0, tiled=True),
        lax.all_gather(qv_bias, "fsdp", axis=0, tiled=True),
        lax.all_gather(out_weight, "fsdp", axis=0, tiled=True),
        lax.all_gather(out_bias, "fsdp", axis=0, tiled=True),
        lax.all_gather(norm1_gain, "fsdp", axis=0, tiled=True),
        lax.all_gather(norm1_bias, "fsdp", axis=0, tiled=True),
    )
    projected = jnp.dot(layer_in, qkv_full, preferred_element_type=jnp.float32)
    qv_vec = qv_full.astype(jnp.float32)
    query_tok = (projected[:, :model_width] + qv_vec[:model_width]).astype(jnp.bfloat16)
    keys_tok = projected[:, model_width : 2 * model_width].astype(jnp.bfloat16)
    values_tok = (projected[:, 2 * model_width :] + qv_vec[model_width:]).astype(jnp.bfloat16)
    heads_query, heads_key, heads_value = (
        lax.all_to_all(query_tok, "seq", split_axis=1, concat_axis=0, tiled=True),
        lax.all_to_all(keys_tok, "seq", split_axis=1, concat_axis=0, tiled=True),
        lax.all_to_all(values_tok, "seq", split_axis=1, concat_axis=0, tiled=True),
    )
    heads_query = heads_query.reshape(slot_rows, head_count, HEAD)
    heads_key = heads_key.reshape(slot_rows, head_count, HEAD)
    heads_value = heads_value.reshape(slot_rows, head_count, HEAD)
    key_in_slot = jnp.arange(slot_rows, dtype=jnp.int32) < length

    def scores_for(query_block):
        scores = (
            jnp.einsum("qhd,khd->hqk", query_block, heads_key, preferred_element_type=jnp.float32)
            * factor
        )
        return jnp.where(key_in_slot[None, None, :], scores, masked_score)

    def forward_block(block_index):
        query_block = lax.dynamic_slice_in_dim(heads_query, block_index * block_rows, block_rows, 0)
        scores = scores_for(query_block)
        row_max = jnp.max(scores, axis=-1, keepdims=True)
        exponent = jnp.exp(scores - row_max)
        row_sum = jnp.sum(exponent, axis=-1, keepdims=True)
        probs_low = (exponent / row_sum).astype(jnp.bfloat16)
        mixed_block = jnp.einsum(
            "hqk,khd->qhd", probs_low, heads_value, preferred_element_type=jnp.float32
        )
        return (mixed_block.astype(jnp.bfloat16), row_max, row_sum)

    mixed_blocks, row_maxes, row_sums = lax.map(
        forward_block, jnp.arange(block_count, dtype=jnp.int32)
    )
    mixed_heads = mixed_blocks.reshape(slot_rows, head_cols)
    attended = lax.all_to_all(mixed_heads, "seq", split_axis=0, concat_axis=1, tiled=True)
    branch = jnp.dot(attended, out_full, preferred_element_type=jnp.float32) + out_bias_full.astype(
        jnp.float32
    )
    resid_one = layer_in.astype(jnp.float32) + branch
    middle, norm_one_back = jax.vjp(
        normalize, resid_one, gain_one.astype(jnp.float32), shift_one.astype(jnp.float32)
    )
    up_full, up_bias_full, down_full, down_bias_full, gain_two, shift_two = (
        lax.all_gather(up_weight, "fsdp", axis=0, tiled=True),
        lax.all_gather(up_bias, "fsdp", axis=0, tiled=True),
        lax.all_gather(down_weight, "fsdp", axis=0, tiled=True),
        lax.all_gather(down_bias, "fsdp", axis=0, tiled=True),
        lax.all_gather(norm2_gain, "fsdp", axis=0, tiled=True),
        lax.all_gather(norm2_bias, "fsdp", axis=0, tiled=True),
    )
    middle_low = middle.astype(jnp.bfloat16)
    up_pre = jnp.dot(middle_low, up_full, preferred_element_type=jnp.float32) + up_bias_full.astype(
        jnp.float32
    )
    gelu_out, gelu_back = jax.vjp(partial(jax.nn.gelu, approximate=False), up_pre)
    hidden = gelu_out.astype(jnp.bfloat16)
    down_pre = jnp.dot(
        hidden, down_full, preferred_element_type=jnp.float32
    ) + down_bias_full.astype(jnp.float32)
    final, norm_two_back = jax.vjp(
        normalize, middle + down_pre, gain_two.astype(jnp.float32), shift_two.astype(jnp.float32)
    )
    output = jnp.where(in_slot, final, 0.0).astype(jnp.bfloat16)
    grad_final = jnp.where(in_slot, cotangent.astype(jnp.float32), 0.0)
    down_back, up_back = (
        lax.all_gather(down_weight, "fsdp", axis=0, tiled=True),
        lax.all_gather(up_weight, "fsdp", axis=0, tiled=True),
    )
    grad_resid_two, grad_gain_two, grad_shift_two = norm_two_back(grad_final)
    grad_down = grad_resid_two.astype(jnp.bfloat16)
    grad_down_bias = column_sums(grad_down)
    grad_down_weight = over_rows(hidden, grad_down)
    grad_hidden = by_columns(grad_down, down_back)
    (grad_up_pre,) = gelu_back(grad_hidden)
    grad_up = grad_up_pre.astype(jnp.bfloat16)
    grad_up_bias = column_sums(grad_up)
    grad_up_weight = over_rows(middle_low, grad_up)
    grad_middle = grad_resid_two + by_columns(grad_up, up_back)
    grad_resid_one, grad_gain_one, grad_shift_one = norm_one_back(grad_middle)
    out_back, qkv_back = (
        lax.all_gather(out_weight, "fsdp", axis=0, tiled=True),
        lax.all_gather(qkv_weight, "fsdp", axis=0, tiled=True),
    )
    grad_branch = grad_resid_one.astype(jnp.bfloat16)
    grad_out_bias = column_sums(grad_branch)
    grad_out_weight = over_rows(attended, grad_branch)
    grad_attended = by_columns(grad_branch, out_back).astype(jnp.bfloat16)
    grad_heads = lax.all_to_all(grad_attended, "seq", split_axis=1, concat_axis=0, tiled=True)
    grad_heads = grad_heads.reshape(slot_rows, head_count, HEAD)

    def backward_block(carry, block_item):
        key_sum, value_sum = carry
        block_index, row_max, row_sum = block_item
        query_block = lax.dynamic_slice_in_dim(heads_query, block_index * block_rows, block_rows, 0)
        grad_block = lax.dynamic_slice_in_dim(grad_heads, block_index * block_rows, block_rows, 0)
        scores = scores_for(query_block)
        attn_probs = jnp.exp(scores - row_max) / row_sum
        probs_low = attn_probs.astype(jnp.bfloat16)
        grad_probs = jnp.einsum(
            "qhd,khd->hqk", grad_block, heads_value, preferred_element_type=jnp.float32
        )
        row_delta = jnp.sum(grad_probs * attn_probs, axis=-1, keepdims=True)
        grad_scores = (attn_probs * (grad_probs - row_delta)).astype(jnp.bfloat16)
        grad_query = (
            jnp.einsum("hqk,khd->qhd", grad_scores, heads_key, preferred_element_type=jnp.float32)
            * factor
        )
        key_sum = (
            key_sum
            + jnp.einsum(
                "hqk,qhd->khd", grad_scores, query_block, preferred_element_type=jnp.float32
            )
            * factor
        )
        value_sum = value_sum + jnp.einsum(
            "hqk,qhd->khd", probs_low, grad_block, preferred_element_type=jnp.float32
        )
        return ((key_sum, value_sum), grad_query.astype(jnp.bfloat16))

    zero_heads = jnp.zeros((slot_rows, head_count, HEAD), jnp.float32)
    (key_total, value_total), query_blocks = lax.scan(
        backward_block,
        (zero_heads, zero_heads),
        (jnp.arange(block_count, dtype=jnp.int32), row_maxes, row_sums),
    )
    grad_query_heads = query_blocks.reshape(slot_rows, head_cols)
    grad_key_heads = key_total.reshape(slot_rows, head_cols).astype(jnp.bfloat16)
    grad_value_heads = value_total.reshape(slot_rows, head_cols).astype(jnp.bfloat16)
    grad_query_tok, grad_key_tok, grad_value_tok = (
        lax.all_to_all(grad_query_heads, "seq", split_axis=0, concat_axis=1, tiled=True),
        lax.all_to_all(grad_key_heads, "seq", split_axis=0, concat_axis=1, tiled=True),
        lax.all_to_all(grad_value_heads, "seq", split_axis=0, concat_axis=1, tiled=True),
    )
    grad_projected = jnp.concatenate([grad_query_tok, grad_key_tok, grad_value_tok], axis=1)
    grad_qv_bias = jnp.concatenate([column_sums(grad_query_tok), column_sums(grad_value_tok)])
    grad_qkv_weight = over_rows(layer_in, grad_projected)
    grad_layer_in = grad_resid_one + by_columns(grad_projected, qkv_back)
    input_grad = jnp.where(is_memory, 0.0, grad_layer_in)
    grad_read = lax.dot_general(
        read_float,
        grad_layer_in,
        (((0,), (0,)), ((), ())),
        precision=lax.Precision.HIGHEST,
        preferred_element_type=jnp.float32,
    )
    grad_write = lax.dot_general(
        write_float,
        grad_layer_in,
        (((0,), (0,)), ((), ())),
        precision=lax.Precision.HIGHEST,
        preferred_element_type=jnp.float32,
    )
    (
        shard_qkv,
        shard_qv,
        shard_out_w,
        shard_out_b,
        shard_gain_one,
        shard_shift_one,
        shard_up_w,
        shard_up_b,
        shard_down_w,
        shard_down_b,
        shard_gain_two,
        shard_shift_two,
    ) = (
        lax.psum_scatter(grad_qkv_weight, "fsdp", scatter_dimension=0, tiled=True),
        lax.psum_scatter(grad_qv_bias, "fsdp", scatter_dimension=0, tiled=True),
        lax.psum_scatter(grad_out_weight, "fsdp", scatter_dimension=0, tiled=True),
        lax.psum_scatter(grad_out_bias, "fsdp", scatter_dimension=0, tiled=True),
        lax.psum_scatter(grad_gain_one, "fsdp", scatter_dimension=0, tiled=True),
        lax.psum_scatter(grad_shift_one, "fsdp", scatter_dimension=0, tiled=True),
        lax.psum_scatter(grad_up_weight, "fsdp", scatter_dimension=0, tiled=True),
        lax.psum_scatter(grad_up_bias, "fsdp", scatter_dimension=0, tiled=True),
        lax.psum_scatter(grad_down_weight, "fsdp", scatter_dimension=0, tiled=True),
        lax.psum_scatter(grad_down_bias, "fsdp", scatter_dimension=0, tiled=True),
        lax.psum_scatter(grad_gain_two, "fsdp", scatter_dimension=0, tiled=True),
        lax.psum_scatter(grad_shift_two, "fsdp", scatter_dimension=0, tiled=True),
    )
    (
        sum_qkv,
        sum_qv,
        sum_out_w,
        sum_out_b,
        sum_gain_one,
        sum_shift_one,
        sum_up_w,
        sum_up_b,
        sum_down_w,
        sum_down_b,
        sum_gain_two,
        sum_shift_two,
        read_total,
        write_total,
    ) = (
        lax.psum(shard_qkv.astype(jnp.bfloat16), "seq").astype(jnp.float32),
        lax.psum(shard_qv.astype(jnp.bfloat16), "seq").astype(jnp.float32),
        lax.psum(shard_out_w.astype(jnp.bfloat16), "seq").astype(jnp.float32),
        lax.psum(shard_out_b.astype(jnp.bfloat16), "seq").astype(jnp.float32),
        lax.psum(shard_gain_one.astype(jnp.bfloat16), "seq").astype(jnp.float32),
        lax.psum(shard_shift_one.astype(jnp.bfloat16), "seq").astype(jnp.float32),
        lax.psum(shard_up_w.astype(jnp.bfloat16), "seq").astype(jnp.float32),
        lax.psum(shard_up_b.astype(jnp.bfloat16), "seq").astype(jnp.float32),
        lax.psum(shard_down_w.astype(jnp.bfloat16), "seq").astype(jnp.float32),
        lax.psum(shard_down_b.astype(jnp.bfloat16), "seq").astype(jnp.float32),
        lax.psum(shard_gain_two.astype(jnp.bfloat16), "seq").astype(jnp.float32),
        lax.psum(shard_shift_two.astype(jnp.bfloat16), "seq").astype(jnp.float32),
        lax.psum(grad_read.astype(jnp.bfloat16), "seq").astype(jnp.float32),
        lax.psum(grad_write.astype(jnp.bfloat16), "seq").astype(jnp.float32),
    )
    return (
        output,
        input_grad,
        read_total[None],
        write_total[None],
        sum_qkv,
        sum_qv,
        sum_out_w,
        sum_out_b,
        sum_gain_one,
        sum_shift_one,
        sum_up_w,
        sum_up_b,
        sum_down_w,
        sum_down_b,
        sum_gain_two,
        sum_shift_two,
    )


def solution(mesh):
    in_specs = (
        P(("fsdp", "seq"), None),
        P("fsdp", None, None),
        P("fsdp", None, None),
        P("fsdp"),
        P("fsdp", None),
        P("fsdp"),
        P("fsdp", None),
        P("fsdp"),
        P("fsdp"),
        P("fsdp"),
        P("fsdp", None),
        P("fsdp"),
        P("fsdp", None),
        P("fsdp"),
        P("fsdp"),
        P("fsdp"),
        P(("fsdp", "seq"), None),
    )
    out_specs = (
        P(("fsdp", "seq"), None),
        P(("fsdp", "seq"), None),
        P("fsdp", None, None),
        P("fsdp", None, None),
        P("fsdp", None),
        P("fsdp"),
        P("fsdp", None),
        P("fsdp"),
        P("fsdp"),
        P("fsdp"),
        P("fsdp", None),
        P("fsdp"),
        P("fsdp", None),
        P("fsdp"),
        P("fsdp"),
        P("fsdp"),
    )
    return jax.shard_map(
        per_device, mesh=mesh, in_specs=in_specs, out_specs=out_specs, check_vma=False
    )
```

profile of v0, /device:TPU:0, one launch (start us, length us, event | category | flops | bytes accessed | tf_op | source)
XLA Modules:
  0.0 1022.8 jit_solution(4488948586990560364)
XLA Ops:
  18.6 39.7 %all-reduce.16 = (bf16[1536]{0:T(1024)(128)(2,1)S(1)}, bf16[768]{0:T(1024)(128)(2,1)S(1)}, bf16[768]{0:T(1024)(128)(2,1)S(1)}, bf16[768]{0:T(1024)(128)(2,1)S(1)...) all-reduce(bf16[1536]{0:T(1024)(128)(2,1)S(1)} %dynamic-update-slic, ...), channel_id=1, replica_groups=mesh['fsdp'=8,'seq'=4] {'fsdp'}, use_global_device_ids=true, to_apply=%add | all-reduce | flops 6144 | bytes 24576
  60.5 18.2 %all-gather.6.cloned.1.call-done = bf16[768,2304]{1,0:T(8,128)(2,1)} async-done(((bf16[96,2304]{1,0:T(8,128)(2,1)}), bf16[768,2304]{1,0:T(8,128)(2,1)}) %all-gather.6.cloned.1.call-update) | async-done | bytes 3538960 | tf_op jit(solution)/shard_map/all_gather | solution.py:79
  78.8 4.0 fusion.80
  91.0 10.5 %all-to-all-done = bf16[512,4,192]{0,2,1:T(8,128)(2,1)S(1)} async-done(((bf16[512,4,192]{0,2,1:T(8,128)(2,1)}), bf16[512,4,192]{0,2,1:T(8,128)(2,1)S(1)}, u32[]{:S(2)}, u32[]{:S(2)}) %all-to-all-start) | async-done | bytes 786464 | tf_op jit(solution)/shard_map/all_to_all | solution.py:92
  107.7 9.0 all-to-all-done.2
  125.5 6.2 all-to-all-done.1
  136.3 44.2 %while.30 = (s32[]{:T(128)}, bf16[4,512,3,64]{1,3,2,0:T(8,128)(2,1)}, f32[4,3,512,1]{2,1,3,0:T(4,128)S(1)}, f32[4,3,512,1]{2,1,3,0:T(4,128)S(1)}, s32[4]{0:T(128...) while((s32[]{:T(128)}, ...), condition=%wide.region_4.5_spmd.clone, body=%wide.region_1.4_spmd.clone.sunk | while | flops 843152384 | bytes 39787204 | solution.py:120
  143.0 4.3 fusion.133
  154.1 4.3 fusion.133
  165.1 4.3 fusion.133
  176.2 4.3 fusion.133
  184.1 26.3 %all-gather = bf16[8,1,384]{2,1,0:T(2,128)(2,1)S(1)} all-gather(bf16[1,1,384]{2,1,0:T(2,128)(2,1)S(1)} %reshape.204), channel_id=1, replica_groups=mesh['fsdp'=8,'seq'=4] {'fsdp'}, dimensions={0}, use_global_device_ids=true | all-gather | bytes 6912 | tf_op jit(solution)/shard_map/all_gather | solution.py:134
  214.5 20.9 %multiply_convert_fusion.1 = (bf16[512,3072]{1,0:T(8,128)(2,1)}, f32[512,3072]{1,0:T(8,128)}, f32[512,3072]{1,0:T(8,128)}) fusion(f32[3072]{0:T(1024)S(1)} %bitcast.154, bf16[768,3072]{1,0:T(8,128)(2,1)} %all-gather.10.cloned.1.call-done, f32[512,768]{1,0:T(8,128)} %copy-done.7, f32[768]{0:T(1024)S(1)} %convert_element_type.216, ...), kind=kOutput, calls=%fused_computation.49 | convolution fusion | flops 2521694208 | bytes 22042624 | tf_op jit(solution)/shard_map/dot_general | solution.py:141
  235.4 46.2 %all-gather.12.cloned.1.call-done = bf16[3072,768]{1,0:T(8,128)(2,1)} async-done(((bf16[384,768]{1,0:T(8,128)(2,1)}), bf16[3072,768]{1,0:T(8,128)(2,1)}) %all-gather.12.cloned.1.call-update) | async-done | bytes 4718608 | tf_op jit(solution)/shard_map/all_gather | solution.py:135
  281.6 6.1 fusion.79
  292.0 8.9 convert_reduce_fusion
  300.9 3.6 multiply_reduce_fusion.2
  309.1 4.2 all-to-all-start.4
  316.8 8.2 all-to-all-done.4
  331.4 115.4 %while.31 = (s32[]{:T(128)}, f32[2048,3,64]{0,2,1:T(8,128)S(1)}, f32[2048,3,64]{0,2,1:T(8,128)}, bf16[4,512,3,64]{1,3,2,0:T(8,128)(2,1)}, s32[4]{0:T(128)S(1)}, ...) while((s32[]{:T(128)}, f32[2048,3,64]{0,2,1:T(8,128)S(1)}, ...), condition=%wide.region_15.16_spmd.clone, body=%wide.region_13.15_spmd.clone.sunk | while | flops 2046886400 | bytes 204722992 | solution.py:210
  333.4 4.3 exponential_divide_fusion.2
  345.7 4.5 fusion.143
  350.2 6.3 fusion.145
  361.8 4.3 exponential_divide_fusion.2
  374.2 4.5 fusion.143
  378.6 6.3 fusion.145
  385.0 4.0 fusion.144
  390.9 4.3 exponential_divide_fusion.2
  403.2 4.4 fusion.143
  407.7 6.3 fusion.145
  413.9 4.0 fusion.144
  419.8 4.3 exponential_divide_fusion.2
  432.2 4.4 fusion.143
  436.6 6.3 fusion.145
  442.9 4.0 fusion.144
  454.5 9.2 all-to-all-done.6
  463.7 14.1 %all_to_all.134 = bf16[4,512,192]{1,2,0:T(8,128)(2,1)S(1)} all-to-all(bf16[4,512,192]{1,2,0:T(8,128)(2,1)S(1)} %copy.93), channel_id=1, replica_groups=mesh['fsdp'=8,'seq'=4] {'seq'}, dimensions={0} | all-to-all | bytes 1572864 | tf_op jit(solution)/shard_map/all_to_all | solution.py:221
  477.8 14.3 %all_to_all.135 = bf16[4,512,192]{1,2,0:T(8,128)(2,1)S(1)} all-to-all(bf16[4,512,192]{1,2,0:T(8,128)(2,1)S(1)} %bitcast.149), channel_id=1, replica_groups=mesh['fsdp'=8,'seq'=4] {'seq'}, dimensions={0} | all-to-all | bytes 1572864 | tf_op jit(solution)/shard_map/all_to_all | solution.py:219
  492.0 6.4 fusion.51
  499.5 8.2 fusion.82
  509.2 7.2 fusion.69
  519.1 37.6 %all-reduce.15 = (bf16[1536]{0:T(1024)(128)(2,1)S(1)}, bf16[768]{0:T(1024)(128)(2,1)S(1)}, bf16[768]{0:T(1024)(128)(2,1)S(1)}, bf16[768]{0:T(1024)(128)(2,1)S(1)...) all-reduce(f32[1536]{0:T(1024)S(1)} %pad_maximum_fusion.3, ...), channel_id=3, replica_groups=mesh['fsdp'=8,'seq'=4] {'fsdp'}, use_global_device_ids=true, to_apply=%region_22.23.clone | all-reduce | flops 9216 | bytes 55296
  559.2 66.9 %reduce-scatter.5.cloned.1.call-done = f32[96,2304]{1,0:T(8,128)} async-done(((f32[768,2304]{1,0:T(8,128)}), f32[96,2304]{1,0:T(8,128)}) %reduce-scatter.5.cloned.1.call-update) | async-done | bytes 884752 | tf_op jit(solution)/shard_map/reduce_scatter | solution.py:256
  628.1 164.6 %reduce-scatter.11.cloned.1.call-done = f32[384,768]{1,0:T(8,128)} async-done(((f32[3072,768]{1,0:T(8,128)}), f32[384,768]{1,0:T(8,128)}) %reduce-scatter.11.cloned.1.call-update) | async-done | bytes 1179664 | tf_op jit(solution)/shard_map/reduce_scatter | solution.py:264
  794.8 164.3 %reduce-scatter.9.cloned.1.call-done = f32[96,3072]{1,0:T(8,128)} async-done(((f32[768,3072]{1,0:T(8,128)}), f32[96,3072]{1,0:T(8,128)}) %reduce-scatter.9.cloned.1.call-update) | async-done | bytes 1179664 | tf_op jit(solution)/shard_map/reduce_scatter | solution.py:262
  961.4 5.6 broadcast_select_fusion
  968.2 14.3 %all-reduce.17 = (bf16[1,10,768]{2,1,0:T(8,128)(2,1)S(1)}, bf16[1,10,768]{2,1,0:T(8,128)(2,1)S(1)}, bf16[192]{0:T(256)(128)(2,1)S(1)}, bf16[96]{0:T(256)(128)(2,...) all-reduce(bf16[1,10,768]{2,1,0:T(8,128)(2,1)S(1)} %fusion.49, ...), channel_id=1, replica_groups=mesh['fsdp'=8,'seq'=4] {'seq'}, use_global_device_ids=true, to_apply=%region_16.17 | all-reduce | flops 16512 | bytes 66048 | tf_op jit(solution)/shard_map/psum | solution.py:297
  988.0 21.9 %all-reduce.21.cloned.1.call-done = (bf16[96,2304]{1,0:T(8,128)(2,1)}, bf16[96,768]{1,0:T(8,128)(2,1)}, bf16[96,3072]{1,0:T(8,128)(2,1)}, bf16[384,768]{1,0:T(8,128)(2,1)}) async-done(((bf16[96,2304]{1,0:T(8,128)(2,1)}, bf16[96,768]{1,0:T(8,128)(2,1)}, bf16[96,3072]{1,0:T(8,128)(2,1)}, bf16[384,768]{1,0:T(8,128)(2,1)}), (bf16[96,2304]{1,0:T(8,128)(2,1)}, bf16[96,768]{1,0:T(8,128)(2,1)}, ...) | async-done | bytes 1769488 | tf_op jit(solution)/shard_map/psum | solution.py:285
  (292 shorter events, 162.4 us)
Async XLA Ops:
  7.2 51.2 %copy-start = (bf16[1,10,768]{2,1,0:T(8,128)(2,1)S(1)}, bf16[1,10,768]{2,1,0:T(8,128)(2,1)}, u32[]{:S(2)}) copy-start(bf16[1,10,768]{2,1,0:T(8,128)(2,1)} %param.22) | copy-start | bytes 46084
  7.2 71.6 %all-gather.6.cloned.1.call-start = ((), (), s32[]{:S(2)}) async-start(), calls=%async_computation.12 | async-start | bytes 3981312 | tf_op jit(solution)/shard_map/all_gather | solution.py:79
  7.9 202.6 %all-gather.8.cloned.1.call-start = ((), (), s32[]{:S(2)}) async-start(), calls=%async_computation.13 | async-start | bytes 1327104 | tf_op jit(solution)/shard_map/all_gather | solution.py:81
  8.7 205.8 %all-gather.10.cloned.1.call-start = ((), (), s32[]{:S(2)}) async-start(), calls=%async_computation.14 | async-start | bytes 5308416 | tf_op jit(solution)/shard_map/all_gather | solution.py:133
  58.3 24.5 %copy-start.37 = (s32[10]{0:T(128)}, s32[10]{0:T(128)S(1)}, u32[]{:S(2)}) copy-start(s32[10]{0:T(128)S(1)} %iota_add_fusion.1) | copy-start | bytes 124
  58.4 24.4 %copy-start.43 = (pred[512]{0:T(512)(128)(4,1)}, pred[512]{0:T(512)(128)(4,1)S(1)}, u32[]{:S(2)}) copy-start(pred[512]{0:T(512)(128)(4,1)S(1)} %fusion.54) | copy-start | bytes 1540
  60.5 22.3 %copy-start.17 = (bf16[512,768]{1,0:T(8,128)(2,1)}, bf16[512,768]{1,0:T(8,128)(2,1)S(1)}, u32[]{:S(2)}) copy-start(bf16[512,768]{1,0:T(8,128)(2,1)S(1)} %fusion.47) | copy-start | bytes 2359300
  86.4 15.1 %all-to-all-start = ((bf16[512,4,192]{0,2,1:T(8,128)(2,1)}), bf16[512,4,192]{0,2,1:T(8,128)(2,1)S(1)}, u32[]{:S(2)}, u32[]{:S(2)}) async-start(bf16[512,4,192]{0,2,1:T(8,128)(2,1)} %bitcast.4), calls=%async_computation | async-start | bytes 1572864 | tf_op jit(solution)/shard_map/all_to_all | solution.py:92
  101.5 15.1 %all-to-all-start.2 = ((bf16[512,4,192]{0,2,1:T(8,128)(2,1)}), bf16[512,4,192]{0,2,1:T(8,128)(2,1)S(1)}, u32[]{:S(2)}, u32[]{:S(2)}) async-start(bf16[512,4,192]{0,2,1:T(8,128)(2,1)} %bitcast.8), calls=%async_computation.2 | async-start | bytes 1572864 | tf_op jit(solution)/shard_map/all_to_all | solution.py:94
  116.6 15.1 %all-to-all-start.1 = ((bf16[512,4,192]{0,2,1:T(8,128)(2,1)}), bf16[512,4,192]{0,2,1:T(8,128)(2,1)S(1)}, u32[]{:S(2)}, u32[]{:S(2)}) async-start(bf16[512,4,192]{0,2,1:T(8,128)(2,1)} %bitcast.6), calls=%async_computation.1 | async-start | bytes 1572864 | tf_op jit(solution)/shard_map/all_to_all | solution.py:93
  120.1 161.5 %all-gather.12.cloned.1.call-start = ((), (), s32[]{:S(2)}) async-start(), calls=%async_computation.15 | async-start | bytes 5308416 | tf_op jit(solution)/shard_map/all_gather | solution.py:135
  136.3 47.7 %copy-start.45 = (bf16[384]{0:T(512)(128)(2,1)S(1)}, bf16[384]{0:T(512)(128)(2,1)}, u32[]{:S(2)}) copy-start(bf16[384]{0:T(512)(128)(2,1)} %param.32) | copy-start | bytes 2308
  180.5 34.0 %copy-start.4 = (bf16[2048,3,64]{0,2,1:T(8,128)(2,1)}, bf16[2048,3,64]{0,2,1:T(8,128)(2,1)S(1)}, u32[]{:S(2)}) copy-start(bf16[2048,3,64]{0,2,1:T(8,128)(2,1)S(1)} %get-tuple-element.654) | copy-start | bytes 2359300
  180.5 34.0 %copy-start.6 = (bf16[2048,3,64]{0,2,1:T(8,128)(2,1)}, bf16[2048,3,64]{0,2,1:T(8,128)(2,1)S(1)}, u32[]{:S(2)}) copy-start(bf16[2048,3,64]{0,2,1:T(8,128)(2,1)S(1)} %get-tuple-element.655) | copy-start | bytes 2359300
  180.5 30.0 %all-to-all-start.3 = ((bf16[4,512,192]{1,2,0:T(8,128)(2,1)}), bf16[4,512,192]{1,2,0:T(8,128)(2,1)S(1)}, u32[]{:S(2)}, u32[]{:S(2)}) async-start(bf16[4,512,192]{1,2,0:T(8,128)(2,1)} %bitcast.10), calls=%async_computation.3 | async-start | bytes 1572864 | tf_op jit(solution)/shard_map/all_to_all | solution.py:124
  184.0 120.5 %copy-start.30 = (f32[768]{0:T(1024)}, f32[768]{0:T(1024)S(1)}, u32[]{:S(2)}) copy-start(f32[768]{0:T(1024)S(1)} %convert_element_type.215) | copy-start | bytes 9220
  184.1 97.5 %copy-start.39 = (f32[768]{0:T(1024)}, f32[768]{0:T(1024)S(1)}, u32[]{:S(2)}) copy-start(f32[768]{0:T(1024)S(1)} %convert_element_type.216) | copy-start | bytes 9220
  213.0 91.5 %copy-start.24 = (f32[512]{0:T(512)}, f32[512]{0:T(512)S(1)}, u32[]{:S(2)}) copy-start(f32[512]{0:T(512)S(1)} %broadcast_multiply_fusion.1) | copy-start | bytes 6148
  214.5 90.1 %copy-start.33 = (f32[512]{0:T(512)}, f32[512]{0:T(512)S(1)}, u32[]{:S(2)}) copy-start(f32[512]{0:T(512)S(1)} %fusion.65) | copy-start | bytes 6148
  214.5 67.1 %copy-start.8 = (f32[512,768]{1,0:T(8,128)S(1)}, f32[512,768]{1,0:T(8,128)}, u32[]{:S(2)}) copy-start(f32[512,768]{1,0:T(8,128)} %copy-done.7) | copy-start | bytes 4718596
  281.6 6.5 copy-start.13
  291.1 9.8 slice-start
  291.9 9.0 copy-start.18
  292.0 8.9 slice-start.1
  307.2 6.2 copy-start.15
  309.1 15.9 %all-to-all-start.4 = ((bf16[512,4,192]{0,2,1:T(8,128)(2,1)}), bf16[512,4,192]{0,2,1:T(8,128)(2,1)}, u32[]{:S(2)}, u32[]{:S(2)}) async-start(bf16[512,4,192]{0,2,1:T(8,128)(2,1)} %bitcast.15), calls=%async_computation.4 | async-start | bytes 1572864 | tf_op jit(solution)/shard_map/all_to_all | solution.py:177
  313.4 244.0 %reduce-scatter.7.cloned.1.call-start = ((), (), s32[]{:S(2)}) async-start(), calls=%async_computation.17 | async-start | bytes 2654208 | tf_op jit(solution)/shard_map/reduce_scatter | solution.py:258
  316.8 14.6 %copy-start.5 = (bf16[2048,3,64]{0,2,1:T(8,128)(2,1)S(1)}, bf16[2048,3,64]{0,2,1:T(8,128)(2,1)}, u32[]{:S(2)}) copy-start(bf16[2048,3,64]{0,2,1:T(8,128)(2,1)} %copy-done.4) | copy-start | bytes 2359300
  337.7 4.5 copy-start.2
  345.7 10.8 %copy-start.3 = (f32[3,512,2048]{2,1,0:T(8,128)S(1)}, f32[3,512,2048]{2,1,0:T(8,128)}, u32[]{:S(2)}) copy-start(f32[3,512,2048]{2,1,0:T(8,128)} %copy-done.2) | copy-start | bytes 37748740 | tf_op jit(solution)/shard_map/while
  374.2 10.8 %copy-start.3 = (f32[3,512,2048]{2,1,0:T(8,128)S(1)}, f32[3,512,2048]{2,1,0:T(8,128)}, u32[]{:S(2)}) copy-start(f32[3,512,2048]{2,1,0:T(8,128)} %copy-done.2) | copy-start | bytes 37748740 | tf_op jit(solution)/shard_map/while
  395.2 4.5 copy-start.2
  403.2 10.7 %copy-start.3 = (f32[3,512,2048]{2,1,0:T(8,128)S(1)}, f32[3,512,2048]{2,1,0:T(8,128)}, u32[]{:S(2)}) copy-start(f32[3,512,2048]{2,1,0:T(8,128)} %copy-done.2) | copy-start | bytes 37748740 | tf_op jit(solution)/shard_map/while
  432.2 10.7 %copy-start.3 = (f32[3,512,2048]{2,1,0:T(8,128)S(1)}, f32[3,512,2048]{2,1,0:T(8,128)}, u32[]{:S(2)}) copy-start(f32[3,512,2048]{2,1,0:T(8,128)} %copy-done.2) | copy-start | bytes 37748740 | tf_op jit(solution)/shard_map/while
  448.6 15.1 %all-to-all-start.6 = ((bf16[4,512,192]{1,2,0:T(8,128)(2,1)}), bf16[4,512,192]{1,2,0:T(8,128)(2,1)S(1)}, u32[]{:S(2)}, u32[]{:S(2)}) async-start(bf16[4,512,192]{1,2,0:T(8,128)(2,1)} %copy.92), calls=%async_computation.6 | async-start | bytes 1572864 | tf_op jit(solution)/shard_map/all_to_all | solution.py:220
  452.1 174.0 %reduce-scatter.5.cloned.1.call-start = ((), (), s32[]{:S(2)}) async-start(), calls=%async_computation.16 | async-start | bytes 7962624 | tf_op jit(solution)/shard_map/reduce_scatter | solution.py:256
  452.1 25.6 %copy-start.14 = (bf16[4,512,3,64]{1,3,2,0:T(8,128)(2,1)S(1)}, bf16[4,512,3,64]{1,3,2,0:T(8,128)(2,1)}, u32[]{:S(2)}) copy-start(bf16[4,512,3,64]{1,3,2,0:T(8,128)(2,1)} %get-tuple-element.132) | copy-start | bytes 2359300
  463.7 14.1 %copy-start.16 = (bf16[4,512,192]{1,2,0:T(8,128)(2,1)}, bf16[4,512,192]{1,2,0:T(8,128)(2,1)S(1)}, u32[]{:S(2)}) copy-start(bf16[4,512,192]{1,2,0:T(8,128)(2,1)S(1)} %all-to-all-done.6) | copy-start | bytes 2359300
  498.4 294.3 %reduce-scatter.11.cloned.1.call-start = ((), (), s32[]{:S(2)}) async-start(), calls=%async_computation.19 | async-start | bytes 10616832 | tf_op jit(solution)/shard_map/reduce_scatter | solution.py:264
  507.8 451.4 %reduce-scatter.9.cloned.1.call-start = ((), (), s32[]{:S(2)}) async-start(), calls=%async_computation.18 | async-start | bytes 10616832 | tf_op jit(solution)/shard_map/reduce_scatter | solution.py:262
  516.5 493.4 %all-reduce.21.cloned.1.call-start = ((), (), s32[]{:S(2)}) async-start(), calls=%async_computation.20 | async-start | bytes 3538944 | tf_op jit(solution)/shard_map/psum | solution.py:285
  557.4 404.0 %copy-start.11 = (f32[512,768]{1,0:T(8,128)S(1)}, f32[512,768]{1,0:T(8,128)}, u32[]{:S(2)}) copy-start(f32[512,768]{1,0:T(8,128)} %copy-done.10) | copy-start | bytes 4718596
  557.4 404.0 %copy-start.36 = (f32[512]{0:T(512)S(1)}, f32[512]{0:T(512)}, u32[]{:S(2)}) copy-start(f32[512]{0:T(512)} %copy-done.35) | copy-start | bytes 6148
  557.4 404.0 %copy-start.44 = (pred[512]{0:T(512)(128)(4,1)S(1)}, pred[512]{0:T(512)(128)(4,1)}, u32[]{:S(2)}) copy-start(pred[512]{0:T(512)(128)(4,1)} %copy-done.43) | copy-start | bytes 1540
  961.4 5.6 copy-start.23
  961.4 6.2 copy-start.38
  967.0 49.1 %copy-start.1 = (bf16[1,10,768]{2,1,0:T(8,128)(2,1)S(1)}, bf16[1,10,768]{2,1,0:T(8,128)(2,1)}, u32[]{:S(2)}) copy-start(bf16[1,10,768]{2,1,0:T(8,128)(2,1)} %param.22) | copy-start | bytes 46084
  1009.9 5.4 copy-start.21
  (24 other events, 58.3 us)
Sparse Core Ops, SparseCore 0:
  10.2 68.4 all-gather.5
  80.9 39.4 all-gather.7
  122.7 78.6 all-gather.9
  203.4 78.1 all-gather.11
  317.4 67.6 reduce-scatter.6
  498.5 127.5 reduce-scatter.4
  630.1 162.5 reduce-scatter.10
  796.7 162.3 reduce-scatter.8
  963.1 46.7 all-reduce.20
where the time goes:
time: 1030 us; the launch traced here: 1020 us
  waiting for transfers between devices  528 us (51%)
  matrix products  195 us (19%)
  blocking collectives  146 us (14%)
  other arithmetic  57.2 us (6%)
  local copies, waits for them, and re-layouts  50.3 us (5%)
  starting transfers between devices  22.2 us (2%)
  between operations  18.7 us (2%)
    reduce_scatter x1, waiting for transfers between devices, per_device(): lax.psum_scatter(grad_down_weight, 'fsdp', scatter_dimension=0, tiled=True)  165 us
    reduce_scatter x1, waiting for transfers between devices, per_device(): lax.psum_scatter(grad_up_weight, 'fsdp', scatter_dimension=0, tiled=True)  164 us
    unnamed x2, blocking collectives  77.3 us
    reduce_scatter x1, waiting for transfers between devices, per_device(): lax.psum_scatter(grad_qkv_weight, 'fsdp', scatter_dimension=0, tiled=True)  66.9 us
    all_gather x1, waiting for transfers between devices, per_device(): lax.all_gather(down_weight, 'fsdp', axis=0, tiled=True)  46.2 us
    all_gather x1, blocking collectives, per_device(): lax.all_gather(up_bias, 'fsdp', axis=0, tiled=True)  26.3 us
    dot_general x8, matrix products, scores_for(): jnp.einsum('qhd,khd->hqk', query_block, heads_key, preferred_element_type...  25.4 us
    dot_general x4, matrix products, over_rows(): lax.dot_general(left, right, (((0,), (0,)), ((), ())), preferred_element_...  25.2 us
  transfers between devices with their start and end apart: 15, of which 11 were waited for; matrix products, arithmetic and copies ran while one was open for 25% of the time, Pallas kernels for 0%

commit v1 on v0

--- a/solution.py
+++ b/solution.py
@@ -282,7 +282,7 @@
         read_total,
         write_total,
     ) = (
-        lax.psum(shard_qkv.astype(jnp.bfloat16), "seq").astype(jnp.float32),
+        jnp.sum(lax.all_gather(shard_qkv.astype(jnp.bfloat16), "seq"), axis=0).astype(jnp.float32),
         lax.psum(shard_qv.astype(jnp.bfloat16), "seq").astype(jnp.float32),
         lax.psum(shard_out_w.astype(jnp.bfloat16), "seq").astype(jnp.float32),
         lax.psum(shard_out_b.astype(jnp.bfloat16), "seq").astype(jnp.float32),

time: 1030 us -> 1110 us (1.078)
  waiting for transfers between devices: 528 us -> 616 us
    reduce_scatter x1, waiting for transfers between devices: 0.01 us -> 61.7 us  [per_device(): lax.psum_scatter(grad_out_weight, 'fsdp', scatter_dimension=0, tiled=True)]
    reduce_scatter x1, waiting for transfers between devices: 66.9 us -> 105 us  [per_device(): lax.psum_scatter(grad_qkv_weight, 'fsdp', scatter_dimension=0, tiled=True)]
    psum x1, waiting for transfers between devices: 21.9 us -> 6.17 us  [per_device(): lax.psum(shard_out_w.astype(jnp.bfloat16), 'seq').astype(jnp.float32)]
  transfers between devices with their start and end apart: 15 -> 16, of which waited for: 11 -> 12; matrix products, arithmetic and copies ran while one was open for 25% -> 13% of each run, Pallas kernels for 0% -> 0%
where the time goes in v1:
time: 1110 us
  waiting for transfers between devices  616 us (55%)
  matrix products  195 us (18%)
  blocking collectives  140 us (13%)
  other arithmetic  59.1 us (5%)
  local copies, waits for them, and re-layouts  51.2 us (5%)
  starting transfers between devices  22.2 us (2%)
  between operations  19.1 us (2%)
    reduce_scatter x1, waiting for transfers between devices, per_device(): lax.psum_scatter(grad_down_weight, 'fsdp', scatter_dimension=0, tiled=True)  165 us
    reduce_scatter x1, waiting for transfers between devices, per_device(): lax.psum_scatter(grad_up_weight, 'fsdp', scatter_dimension=0, tiled=True)  164 us
    reduce_scatter x1, waiting for transfers between devices, per_device(): lax.psum_scatter(grad_qkv_weight, 'fsdp', scatter_dimension=0, tiled=True)  105 us
    unnamed x2, blocking collectives  75.3 us
    reduce_scatter x1, waiting for transfers between devices, per_device(): lax.psum_scatter(grad_out_weight, 'fsdp', scatter_dimension=0, tiled=True)  61.7 us
    all_gather x1, waiting for transfers between devices, per_device(): lax.all_gather(down_weight, 'fsdp', axis=0, tiled=True)  46 us
    all_gather x1, blocking collectives, per_device(): lax.all_gather(up_bias, 'fsdp', axis=0, tiled=True)  26.1 us
    dot_general x8, matrix products, scores_for(): jnp.einsum('qhd,khd->hqk', query_block, heads_key, preferred_element_type...  25.4 us
  transfers between devices with their start and end apart: 16, of which 12 were waited for; matrix products, arithmetic and copies ran while one was open for 13% of the time, Pallas kernels for 0%

profile of v1, /device:TPU:0, one launch (start us, length us, event | category | flops | bytes accessed | tf_op | source)
XLA Modules:
  0.0 1108.4 jit_solution(4016758210707672629)
XLA Ops:
  18.6 39.7 %all-reduce.16 = (bf16[1536]{0:T(1024)(128)(2,1)S(1)}, bf16[768]{0:T(1024)(128)(2,1)S(1)}, bf16[768]{0:T(1024)(128)(2,1)S(1)}, bf16[768]{0:T(1024)(128)(2,1)S(1)...) all-reduce(bf16[1536]{0:T(1024)(128)(2,1)S(1)} %dynamic-update-slic, ...), channel_id=1, replica_groups=mesh['fsdp'=8,'seq'=4] {'fsdp'}, use_global_device_ids=true, to_apply=%add | all-reduce | flops 6144 | bytes 24576
  60.5 18.2 %all-gather.8.cloned.1.call-done = bf16[768,2304]{1,0:T(8,128)(2,1)} async-done(((bf16[96,2304]{1,0:T(8,128)(2,1)}), bf16[768,2304]{1,0:T(8,128)(2,1)}) %all-gather.8.cloned.1.call-update) | async-done | bytes 3538960 | tf_op jit(solution)/shard_map/all_gather | solution.py:79
  78.8 4.0 fusion.80
  91.0 10.5 all-to-all-done
  107.6 9.0 all-to-all-done.2
  125.5 6.2 all-to-all-done.1
  136.3 44.2 %while.30 = (s32[]{:T(128)}, bf16[4,512,3,64]{1,3,2,0:T(8,128)(2,1)}, f32[4,3,512,1]{2,1,3,0:T(4,128)S(1)}, f32[4,3,512,1]{2,1,3,0:T(4,128)S(1)}, s32[4]{0:T(128...) while((s32[]{:T(128)}, ...), condition=%wide.region_4.5_spmd.clone, body=%wide.region_1.4_spmd.clone.sunk | while | flops 843152384 | bytes 39787204 | solution.py:120
  143.0 4.3 fusion.133
  154.1 4.3 fusion.133
  165.1 4.3 fusion.133
  176.2 4.3 fusion.133
  184.1 26.1 %all-gather.1 = bf16[8,1,384]{2,1,0:T(2,128)(2,1)S(1)} all-gather(bf16[1,1,384]{2,1,0:T(2,128)(2,1)S(1)} %reshape.205), channel_id=1, replica_groups=mesh['fsdp'=8,'seq'=4] {'fsdp'}, dimensions={0}, use_global_device_ids=true | all-gather | bytes 6912 | tf_op jit(solution)/shard_map/all_gather | solution.py:134
  214.6 21.0 %multiply_convert_fusion.1 = (bf16[512,3072]{1,0:T(8,128)(2,1)}, f32[512,3072]{1,0:T(8,128)}, f32[512,3072]{1,0:T(8,128)}) fusion(f32[3072]{0:T(1024)S(1)} %bitcast.156, bf16[768,3072]{1,0:T(8,128)(2,1)} %all-gather.12.cloned.1.call-done, f32[512,768]{1,0:T(8,128)} %copy-done.7, f32[768]{0:T(1024)S(1)} %convert_element_type.218, ...), kind=kOutput, calls=%fused_computation.49 | convolution fusion | flops 2521694208 | bytes 22042624 | tf_op jit(solution)/shard_map/dot_general | solution.py:141
  235.6 46.0 %all-gather.14.cloned.1.call-done = bf16[3072,768]{1,0:T(8,128)(2,1)} async-done(((bf16[384,768]{1,0:T(8,128)(2,1)}), bf16[3072,768]{1,0:T(8,128)(2,1)}) %all-gather.14.cloned.1.call-update) | async-done | bytes 4718608 | tf_op jit(solution)/shard_map/all_gather | solution.py:135
  281.6 6.1 fusion.79
  292.0 9.2 convert_reduce_fusion
  309.4 4.2 all-to-all-start.4
  313.6 11.7 %all-to-all-done.4 = bf16[512,4,192]{0,2,1:T(8,128)(2,1)} async-done(((bf16[512,4,192]{0,2,1:T(8,128)(2,1)}), bf16[512,4,192]{0,2,1:T(8,128)(2,1)}, u32[]{:S(2)}, u32[]{:S(2)}) %all-to-all-start.4) | async-done | bytes 786464 | tf_op jit(solution)/shard_map/all_to_all | solution.py:177
  331.7 115.5 %while.31 = (s32[]{:T(128)}, f32[2048,3,64]{0,2,1:T(8,128)S(1)}, f32[2048,3,64]{0,2,1:T(8,128)}, bf16[4,512,3,64]{1,3,2,0:T(8,128)(2,1)}, s32[4]{0:T(128)S(1)}, ...) while((s32[]{:T(128)}, f32[2048,3,64]{0,2,1:T(8,128)S(1)}, ...), condition=%wide.region_15.16_spmd.clone, body=%wide.region_13.15_spmd.clone.sunk | while | flops 2046886400 | bytes 204722992 | solution.py:210
  333.6 4.3 exponential_divide_fusion.2
  346.0 4.4 fusion.143
  350.4 6.3 fusion.145
  362.0 4.3 exponential_divide_fusion.2
  374.4 4.4 fusion.143
  378.8 6.3 fusion.145
  385.1 4.0 fusion.144
  391.0 4.3 exponential_divide_fusion.2
  403.4 4.4 fusion.143
  407.8 6.3 fusion.145
  414.1 4.0 fusion.144
  420.1 4.3 exponential_divide_fusion.2
  432.4 4.4 fusion.143
  436.9 6.3 fusion.145
  443.1 4.0 fusion.144
  454.8 9.2 all-to-all-done.6
  464.0 14.1 %all_to_all.134 = bf16[4,512,192]{1,2,0:T(8,128)(2,1)S(1)} all-to-all(bf16[4,512,192]{1,2,0:T(8,128)(2,1)S(1)} %copy.93), channel_id=1, replica_groups=mesh['fsdp'=8,'seq'=4] {'seq'}, dimensions={0} | all-to-all | bytes 1572864 | tf_op jit(solution)/shard_map/all_to_all | solution.py:221
  478.1 14.2 %all_to_all.135 = bf16[4,512,192]{1,2,0:T(8,128)(2,1)S(1)} all-to-all(bf16[4,512,192]{1,2,0:T(8,128)(2,1)S(1)} %bitcast.150), channel_id=1, replica_groups=mesh['fsdp'=8,'seq'=4] {'seq'}, dimensions={0} | all-to-all | bytes 1572864 | tf_op jit(solution)/shard_map/all_to_all | solution.py:219
  493.2 6.1 fusion.51
  503.0 8.8 fusion.82
  513.2 7.2 fusion.69
  520.5 105.3 %reduce-scatter.5.cloned.1.call-done = f32[96,2304]{1,0:T(8,128)} async-done(((f32[768,2304]{1,0:T(8,128)}), f32[96,2304]{1,0:T(8,128)}) %reduce-scatter.5.cloned.1.call-update) | async-done | bytes 884752 | tf_op jit(solution)/shard_map/reduce_scatter | solution.py:256
  629.8 6.0 broadcast_select_fusion
  635.9 61.7 %reduce-scatter.7.cloned.1.call-done = f32[96,768]{1,0:T(8,128)} async-done(((f32[768,768]{1,0:T(8,128)}), f32[96,768]{1,0:T(8,128)}) %reduce-scatter.7.cloned.1.call-update) | async-done | bytes 294928 | tf_op jit(solution)/shard_map/reduce_scatter | solution.py:258
  699.2 164.9 %reduce-scatter.11.cloned.1.call-done = f32[384,768]{1,0:T(8,128)} async-done(((f32[3072,768]{1,0:T(8,128)}), f32[384,768]{1,0:T(8,128)}) %reduce-scatter.11.cloned.1.call-update) | async-done | bytes 1179664 | tf_op jit(solution)/shard_map/reduce_scatter | solution.py:264
  866.3 164.5 %reduce-scatter.9.cloned.1.call-done = f32[96,3072]{1,0:T(8,128)} async-done(((f32[768,3072]{1,0:T(8,128)}), f32[96,3072]{1,0:T(8,128)}) %reduce-scatter.9.cloned.1.call-update) | async-done | bytes 1179664 | tf_op jit(solution)/shard_map/reduce_scatter | solution.py:262
  1033.6 35.6 %all-reduce.15 = (bf16[1536]{0:T(1024)(128)(2,1)S(1)}, bf16[768]{0:T(1024)(128)(2,1)S(1)}, bf16[768]{0:T(1024)(128)(2,1)S(1)}, bf16[768]{0:T(1024)(128)(2,1)S(1)...) all-reduce(f32[1536]{0:T(1024)S(1)} %pad_maximum_fusion.3, ...), channel_id=4, replica_groups=mesh['fsdp'=8,'seq'=4] {'fsdp'}, use_global_device_ids=true, to_apply=%region_22.23.clone | all-reduce | flops 9216 | bytes 55296
  1071.1 10.7 all-reduce.17
  1090.1 6.2 all-reduce.21.cloned.1.call-done
  (308 shorter events, 168.0 us)
Async XLA Ops:
  7.2 51.2 %copy-start = (bf16[1,10,768]{2,1,0:T(8,128)(2,1)S(1)}, bf16[1,10,768]{2,1,0:T(8,128)(2,1)}, u32[]{:S(2)}) copy-start(bf16[1,10,768]{2,1,0:T(8,128)(2,1)} %param.22) | copy-start | bytes 46084
  7.2 71.6 %all-gather.8.cloned.1.call-start = ((), (), s32[]{:S(2)}) async-start(), calls=%async_computation.12 | async-start | bytes 3981312 | tf_op jit(solution)/shard_map/all_gather | solution.py:79
  7.9 202.4 %all-gather.10.cloned.1.call-start = ((), (), s32[]{:S(2)}) async-start(), calls=%async_computation.13 | async-start | bytes 1327104 | tf_op jit(solution)/shard_map/all_gather | solution.py:81
  8.7 205.9 %all-gather.12.cloned.1.call-start = ((), (), s32[]{:S(2)}) async-start(), calls=%async_computation.14 | async-start | bytes 5308416 | tf_op jit(solution)/shard_map/all_gather | solution.py:133
  58.3 24.5 %copy-start.43 = (s32[10]{0:T(128)}, s32[10]{0:T(128)S(1)}, u32[]{:S(2)}) copy-start(s32[10]{0:T(128)S(1)} %iota_add_fusion.1) | copy-start | bytes 124
  58.4 24.4 %copy-start.49 = (pred[512]{0:T(512)(128)(4,1)}, pred[512]{0:T(512)(128)(4,1)S(1)}, u32[]{:S(2)}) copy-start(pred[512]{0:T(512)(128)(4,1)S(1)} %fusion.54) | copy-start | bytes 1540
  60.5 22.3 %copy-start.24 = (bf16[512,768]{1,0:T(8,128)(2,1)}, bf16[512,768]{1,0:T(8,128)(2,1)S(1)}, u32[]{:S(2)}) copy-start(bf16[512,768]{1,0:T(8,128)(2,1)S(1)} %fusion.47) | copy-start | bytes 2359300
  86.4 15.1 %all-to-all-start = ((bf16[512,4,192]{0,2,1:T(8,128)(2,1)}), bf16[512,4,192]{0,2,1:T(8,128)(2,1)S(1)}, u32[]{:S(2)}, u32[]{:S(2)}) async-start(bf16[512,4,192]{0,2,1:T(8,128)(2,1)} %bitcast.4), calls=%async_computation | async-start | bytes 1572864 | tf_op jit(solution)/shard_map/all_to_all | solution.py:92
  101.5 15.1 %all-to-all-start.2 = ((bf16[512,4,192]{0,2,1:T(8,128)(2,1)}), bf16[512,4,192]{0,2,1:T(8,128)(2,1)S(1)}, u32[]{:S(2)}, u32[]{:S(2)}) async-start(bf16[512,4,192]{0,2,1:T(8,128)(2,1)} %bitcast.8), calls=%async_computation.2 | async-start | bytes 1572864 | tf_op jit(solution)/shard_map/all_to_all | solution.py:94
  116.6 15.1 %all-to-all-start.1 = ((bf16[512,4,192]{0,2,1:T(8,128)(2,1)}), bf16[512,4,192]{0,2,1:T(8,128)(2,1)S(1)}, u32[]{:S(2)}, u32[]{:S(2)}) async-start(bf16[512,4,192]{0,2,1:T(8,128)(2,1)} %bitcast.6), calls=%async_computation.1 | async-start | bytes 1572864 | tf_op jit(solution)/shard_map/all_to_all | solution.py:93
  120.1 161.5 %all-gather.14.cloned.1.call-start = ((), (), s32[]{:S(2)}) async-start(), calls=%async_computation.15 | async-start | bytes 5308416 | tf_op jit(solution)/shard_map/all_gather | solution.py:135
  136.3 47.7 %copy-start.51 = (bf16[384]{0:T(512)(128)(2,1)S(1)}, bf16[384]{0:T(512)(128)(2,1)}, u32[]{:S(2)}) copy-start(bf16[384]{0:T(512)(128)(2,1)} %param.32) | copy-start | bytes 2308
  180.5 34.0 %copy-start.4 = (bf16[2048,3,64]{0,2,1:T(8,128)(2,1)}, bf16[2048,3,64]{0,2,1:T(8,128)(2,1)S(1)}, u32[]{:S(2)}) copy-start(bf16[2048,3,64]{0,2,1:T(8,128)(2,1)S(1)} %get-tuple-element.652) | copy-start | bytes 2359300
  180.5 34.0 %copy-start.6 = (bf16[2048,3,64]{0,2,1:T(8,128)(2,1)}, bf16[2048,3,64]{0,2,1:T(8,128)(2,1)S(1)}, u32[]{:S(2)}) copy-start(bf16[2048,3,64]{0,2,1:T(8,128)(2,1)S(1)} %get-tuple-element.653) | copy-start | bytes 2359300
  180.5 29.8 %all-to-all-start.3 = ((bf16[4,512,192]{1,2,0:T(8,128)(2,1)}), bf16[4,512,192]{1,2,0:T(8,128)(2,1)S(1)}, u32[]{:S(2)}, u32[]{:S(2)}) async-start(bf16[4,512,192]{1,2,0:T(8,128)(2,1)} %bitcast.10), calls=%async_computation.3 | async-start | bytes 1572864 | tf_op jit(solution)/shard_map/all_to_all | solution.py:124
  184.0 120.8 %copy-start.36 = (f32[768]{0:T(1024)}, f32[768]{0:T(1024)S(1)}, u32[]{:S(2)}) copy-start(f32[768]{0:T(1024)S(1)} %convert_element_type.217) | copy-start | bytes 9220
  184.0 97.6 %copy-start.45 = (f32[768]{0:T(1024)}, f32[768]{0:T(1024)S(1)}, u32[]{:S(2)}) copy-start(f32[768]{0:T(1024)S(1)} %convert_element_type.218) | copy-start | bytes 9220
  210.3 25.3 %copy-start.19 = (bf16[4,512,192]{1,2,0:T(8,128)(2,1)}, bf16[4,512,192]{1,2,0:T(8,128)(2,1)S(1)}, u32[]{:S(2)}) copy-start(bf16[4,512,192]{1,2,0:T(8,128)(2,1)S(1)} %all-to-all-done.3) | copy-start | bytes 2359300
  213.1 91.8 %copy-start.30 = (f32[512]{0:T(512)}, f32[512]{0:T(512)S(1)}, u32[]{:S(2)}) copy-start(f32[512]{0:T(512)S(1)} %broadcast_multiply_fusion.1) | copy-start | bytes 6148
  214.5 90.3 %copy-start.39 = (f32[512]{0:T(512)}, f32[512]{0:T(512)S(1)}, u32[]{:S(2)}) copy-start(f32[512]{0:T(512)S(1)} %fusion.65) | copy-start | bytes 6148
  214.6 67.0 %copy-start.8 = (f32[512,768]{1,0:T(8,128)S(1)}, f32[512,768]{1,0:T(8,128)}, u32[]{:S(2)}) copy-start(f32[512,768]{1,0:T(8,128)} %copy-done.7) | copy-start | bytes 4718596
  308.2 23.5 %copy-start.5 = (bf16[2048,3,64]{0,2,1:T(8,128)(2,1)S(1)}, bf16[2048,3,64]{0,2,1:T(8,128)(2,1)}, u32[]{:S(2)}) copy-start(bf16[2048,3,64]{0,2,1:T(8,128)(2,1)} %copy-done.4) | copy-start | bytes 2359300
  309.4 15.9 %all-to-all-start.4 = ((bf16[512,4,192]{0,2,1:T(8,128)(2,1)}), bf16[512,4,192]{0,2,1:T(8,128)(2,1)}, u32[]{:S(2)}, u32[]{:S(2)}) async-start(bf16[512,4,192]{0,2,1:T(8,128)(2,1)} %bitcast.15), calls=%async_computation.4 | async-start | bytes 1572864 | tf_op jit(solution)/shard_map/all_to_all | solution.py:177
  448.9 15.1 %all-to-all-start.6 = ((bf16[4,512,192]{1,2,0:T(8,128)(2,1)}), bf16[4,512,192]{1,2,0:T(8,128)(2,1)S(1)}, u32[]{:S(2)}, u32[]{:S(2)}) async-start(bf16[4,512,192]{1,2,0:T(8,128)(2,1)} %copy.92), calls=%async_computation.6 | async-start | bytes 1572864 | tf_op jit(solution)/shard_map/all_to_all | solution.py:220
  452.4 173.3 %reduce-scatter.5.cloned.1.call-start = ((), (), s32[]{:S(2)}) async-start(), calls=%async_computation.16 | async-start | bytes 7962624 | tf_op jit(solution)/shard_map/reduce_scatter | solution.py:256
  452.4 25.6 %copy-start.18 = (bf16[4,512,3,64]{1,3,2,0:T(8,128)(2,1)S(1)}, bf16[4,512,3,64]{1,3,2,0:T(8,128)(2,1)}, u32[]{:S(2)}) copy-start(bf16[4,512,3,64]{1,3,2,0:T(8,128)(2,1)} %get-tuple-element.132) | copy-start | bytes 2359300
  464.0 35.3 %copy-start.23 = (bf16[4,512,192]{1,2,0:T(8,128)(2,1)}, bf16[4,512,192]{1,2,0:T(8,128)(2,1)S(1)}, u32[]{:S(2)}) copy-start(bf16[4,512,192]{1,2,0:T(8,128)(2,1)S(1)} %all-to-all-done.6) | copy-start | bytes 2359300
  478.1 14.2 %copy-start.16 = (bf16[4,512,192]{1,2,0:T(8,128)(2,1)}, bf16[4,512,192]{1,2,0:T(8,128)(2,1)S(1)}, u32[]{:S(2)}) copy-start(bf16[4,512,192]{1,2,0:T(8,128)(2,1)S(1)} %all_to_all.134) | copy-start | bytes 2359300
  499.3 198.2 %reduce-scatter.7.cloned.1.call-start = ((), (), s32[]{:S(2)}) async-start(), calls=%async_computation.17 | async-start | bytes 2654208 | tf_op jit(solution)/shard_map/reduce_scatter | solution.py:258
  502.9 361.2 %reduce-scatter.11.cloned.1.call-start = ((), (), s32[]{:S(2)}) async-start(), calls=%async_computation.19 | async-start | bytes 10616832 | tf_op jit(solution)/shard_map/reduce_scatter | solution.py:264
  511.8 518.9 %reduce-scatter.9.cloned.1.call-start = ((), (), s32[]{:S(2)}) async-start(), calls=%async_computation.18 | async-start | bytes 10616832 | tf_op jit(solution)/shard_map/reduce_scatter | solution.py:262
  520.4 109.4 %copy-start.11 = (f32[512,768]{1,0:T(8,128)S(1)}, f32[512,768]{1,0:T(8,128)}, u32[]{:S(2)}) copy-start(f32[512,768]{1,0:T(8,128)} %copy-done.10) | copy-start | bytes 4718596
  520.4 109.4 %copy-start.42 = (f32[512]{0:T(512)S(1)}, f32[512]{0:T(512)}, u32[]{:S(2)}) copy-start(f32[512]{0:T(512)} %copy-done.41) | copy-start | bytes 6148
  520.4 109.4 %copy-start.50 = (pred[512]{0:T(512)(128)(4,1)S(1)}, pred[512]{0:T(512)(128)(4,1)}, u32[]{:S(2)}) copy-start(pred[512]{0:T(512)(128)(4,1)} %copy-done.49) | copy-start | bytes 1540
  520.4 566.9 %all-gather.16.cloned.1.call-start = ((), (), s32[]{:S(2)}) async-start(), calls=%async_computation.20 | async-start | bytes 2211840 | tf_op jit(solution)/shard_map/all_gather | solution.py:285
  627.8 468.5 %all-reduce.21.cloned.1.call-start = ((), (), s32[]{:S(2)}) async-start(), calls=%async_computation.21 | async-start | bytes 2654208 | tf_op jit(solution)/shard_map/psum | solution.py:287
  635.8 397.1 %copy-start.17 = (bf16[4,512,192]{1,2,0:T(8,128)(2,1)S(1)}, bf16[4,512,192]{1,2,0:T(8,128)(2,1)}, u32[]{:S(2)}) copy-start(bf16[4,512,192]{1,2,0:T(8,128)(2,1)} %copy-done.16) | copy-start | bytes 2359300
  635.8 397.4 %copy-start.15 = (bf16[4,512,192]{1,2,0:T(8,128)(2,1)S(1)}, bf16[4,512,192]{1,2,0:T(8,128)(2,1)}, u32[]{:S(2)}) copy-start(bf16[4,512,192]{1,2,0:T(8,128)(2,1)} %copy-done.14) | copy-start | bytes 2359300
  635.8 397.7 %copy-start.32 = (f32[768]{0:T(1024)S(1)}, f32[768]{0:T(1024)}, u32[]{:S(2)}) copy-start(f32[768]{0:T(1024)} %get-tuple-element.296) | copy-start | bytes 9220
  635.8 397.7 %copy-start.33 = (f32[768]{0:T(1024)S(1)}, f32[768]{0:T(1024)}, u32[]{:S(2)}) copy-start(f32[768]{0:T(1024)} %get-tuple-element.299) | copy-start | bytes 9220
  635.8 397.7 %copy-start.34 = (f32[768]{0:T(1024)S(1)}, f32[768]{0:T(1024)}, u32[]{:S(2)}) copy-start(f32[768]{0:T(1024)} %get-tuple-element.370) | copy-start | bytes 9220
  635.9 397.7 %copy-start.35 = (f32[768]{0:T(1024)S(1)}, f32[768]{0:T(1024)}, u32[]{:S(2)}) copy-start(f32[768]{0:T(1024)} %get-tuple-element.374) | copy-start | bytes 9220
  635.9 397.7 %copy-start.38 = (f32[3072]{0:T(1024)S(1)}, f32[3072]{0:T(1024)}, u32[]{:S(2)}) copy-start(f32[3072]{0:T(1024)} %get-tuple-element.372) | copy-start | bytes 36868
  635.9 397.7 %copy-start.47 = (f32[768]{0:T(1024)S(1)}, f32[768]{0:T(1024)}, u32[]{:S(2)}) copy-start(f32[768]{0:T(1024)} %get-tuple-element.294) | copy-start | bytes 9220
  635.9 397.7 %copy-start.48 = (f32[768]{0:T(1024)S(1)}, f32[768]{0:T(1024)}, u32[]{:S(2)}) copy-start(f32[768]{0:T(1024)} %get-tuple-element.298) | copy-start | bytes 9220
  635.9 433.9 %copy-start.29 = (s32[512]{0:T(512)S(1)}, s32[512]{0:T(512)}, u32[]{:S(2)}) copy-start(s32[512]{0:T(512)} %copy-done.28) | copy-start | bytes 6148
  866.3 204.2 %copy-start.44 = (s32[10]{0:T(128)S(1)}, s32[10]{0:T(128)}, u32[]{:S(2)}) copy-start(s32[10]{0:T(128)} %copy-done.43) | copy-start | bytes 124
  1087.3 14.1 %copy-start.1 = (bf16[1,10,768]{2,1,0:T(8,128)(2,1)S(1)}, bf16[1,10,768]{2,1,0:T(8,128)(2,1)}, u32[]{:S(2)}) copy-start(bf16[1,10,768]{2,1,0:T(8,128)(2,1)} %param.22) | copy-start | bytes 46084
  (31 other events, 132.9 us)
Sparse Core Ops, SparseCore 0:
  10.2 68.4 all-gather.7
  80.9 39.5 all-gather.9
  122.7 78.6 all-gather.11
  203.4 78.1 all-gather.13
  499.5 126.2 reduce-scatter.4
  629.5 68.0 reduce-scatter.6
  701.6 162.5 reduce-scatter.10
  868.2 162.5 reduce-scatter.8
  1032.4 19.8 all-gather.15
  1056.0 40.1 all-reduce.20
